TPU v7x, 128 devices: a whole 4x4x4 slice. The times are simulated.
128 devices in a mesh: vocab: 8 (over x_lo, y), dp: 8 (over z, core), teacher: 2 (over x_hi).
Axes of the slice: x: 4 (x_hi: 2, x_lo: 2; x = x_hi * 2 + x_lo), y: 4, z: 4, core: 2. Of those that a mesh axis runs over, the one named last changes fastest.
Arguments:
- hidden_states: bfloat16 [2048, 4096], P('teacher'), may hold values from -300 to 300
- head_weight: bfloat16 [4096, 65536], P(None, ('vocab', 'dp')), may hold values from -3 to 3
- teacher_logits: bfloat16 [2048, 65536], P(None, ('vocab', 'dp', 'teacher')), may hold values from -20 to 460
- token_weight: float32 [2048], P('teacher'), may hold values from 2 to 20
Outputs:
- hidden_grad: bfloat16 [2048, 4096], P('teacher', ('vocab', 'dp'))
- weight_grad: bfloat16 [4096, 65536], P('teacher', ('vocab', 'dp'))
All inputs are finite; a program needn't handle non-finite values.
Results may differ from a plain program's by a relative error of at most 0.005.
Values may be sent and summed in bfloat16 or wider, within the bound.
No kernel may reach another device: no remote copies, remote signals or barrier semaphores. Data moves between devices by JAX's collectives and lax.ppermute only.
A program may use at most 192 MiB of HBM per device.

v0:
```python
import jax
import jax.numpy as jnp
from jax import lax
from jax.sharding import PartitionSpec as P


def per_device(hidden_states, head_weight, teacher_logits, token_weight):
    teacher = lax.all_to_all(
        teacher_logits, "teacher", split_axis=0, concat_axis=1, tiled=True
    ).astype(jnp.float32)
    logits = jnp.dot(hidden_states, head_weight, preferred_element_type=jnp.float32)
    student_top = jnp.max(logits, axis=1)
    teacher_top = jnp.max(teacher, axis=1)
    student_top, teacher_top = lax.pmax((student_top, teacher_top), ("vocab", "dp"))
    student_total = jnp.sum(jnp.exp(logits - student_top[:, None]), axis=1)
    teacher_total = jnp.sum(jnp.exp(teacher - teacher_top[:, None]), axis=1)
    student_total, teacher_total = lax.psum((student_total, teacher_total), ("vocab", "dp"))
    student_norm = student_top + jnp.log(student_total)
    teacher_norm = teacher_top + jnp.log(teacher_total)
    logit_grad = (
        token_weight[:, None]
        * (jnp.exp(logits - student_norm[:, None]) - jnp.exp(teacher - teacher_norm[:, None]))
    ).astype(jnp.bfloat16)
    hidden_share = lax.psum_scatter(
        lax.dot_general(
            head_weight, logit_grad, (((1,), (1,)), ((), ())), preferred_element_type=jnp.float32
        ),
        ("vocab", "dp"),
        scatter_dimension=0,
        tiled=True,
    )
    hidden_grad = hidden_share.T.astype(jnp.bfloat16)
    weight_share = lax.psum_scatter(
        lax.dot_general(
            hidden_states, logit_grad, (((0,), (0,)), ((), ())), preferred_element_type=jnp.float32
        ),
        "teacher",
        scatter_dimension=0,
        tiled=True,
    )
    return (hidden_grad, weight_share.astype(jnp.bfloat16))


def solution(mesh):
    return jax.shard_map(
        per_device,
        mesh=mesh,
        in_specs=(
            P("teacher", None),
            P(None, ("vocab", "dp")),
            P(None, ("vocab", "dp", "teacher")),
            P("teacher"),
        ),
        out_specs=(P("teacher", ("vocab", "dp")), P("teacher", ("vocab", "dp"))),
        check_vma=False,
    )
```

profile of v0, /device:TPU:1, one launch (start us, length us, event | category | flops | bytes accessed | tf_op | source)
XLA Modules:
  0.0 890.2 jit_solution(3435739700118504908)
XLA Ops:
  7.2 4.0 copy.9
  11.1 4.8 all-to-all-start
  16.0 0.0 reduce-scatter.7.cloned.1.call-start
  16.0 15.1 %fusion.4 = (f32[1024]{0:T(1024)S(1)}, f32[1024,1024]{0,1:T(8,128)}) fusion(bf16[1024,4096]{1,0:T(8,128)(2,1)} %param.4, bf16[4096,1024]{1,0:T(8,128)(2,1)} %param.5), kind=kOutput, calls=%fused_computation.12 | convolution fusion | flops 8590982144 | bytes 20975616 | tf_op jit(solution)/shard_map/dot_general | solution.py:11
  31.1 0.0 copy-start.2
  31.1 10.4 %all-to-all-done = bf16[2,1024,512]{1,2,0:T(8,128)(2,1)S(1)} async-done(((bf16[2,1024,512]{1,2,0:T(8,128)(2,1)}), bf16[2,1024,512]{1,2,0:T(8,128)(2,1)S(1)}, u32[]{:S(2)}, u32[]{:S(2)}) %all-to-all-start) | async-done | bytes 2097184 | tf_op jit(solution)/shard_map/all_to_all | solution.py:8
  41.4 0.4 reduce_max.24
  41.8 142.9 %all-reduce.1 = (f32[1024]{0:T(1024)S(1)}, f32[1024]{0:T(1024)S(1)}) all-reduce(bf16[1024]{0:T(1024)(128)(2,1)S(1)} %reduce_max.24, f32[1024]{0:T(1024)S(1)} %get-tuple-element.10), channel_id=1, replica_groups=mesh['vocab'=8,'dp'=8,'teacher'=2] {'vocab','dp'}, use_global_device_ids=true, to_apply=%region_5.0 | all-reduce | flops 2048 | bytes 14336 | tf_op jit(solution)/shard_map/pmax | solution.py:14
  184.7 2.8 exponential_reduce_fusion.1
  187.6 0.7 exponential_reduce_fusion
  188.3 145.1 %all-reduce = (f32[1024]{0:T(1024)S(1)}, f32[1024]{0:T(1024)S(1)}) all-reduce(f32[1024]{0:T(1024)S(1)} %exponential_reduce_fusion, f32[1024]{0:T(1024)S(1)} %exponential_reduce_fusion.1), channel_id=1, replica_groups=mesh['vocab'=8,'dp'=8,'teacher'=2] {'vocab','dp'}, use_global_device_ids=true, to_apply=%region_7.0 | all-reduce | flops 2048 | bytes 16384 | tf_op jit(solution)/shard_map/psum | solution.py:17
  333.4 0.0 copy-done.2
  333.4 3.5 fusion.3
  336.9 0.0 copy-start
  336.9 1.3 copy-done
  338.2 14.5 %convolution_bitcast_fusion.1 = f32[4096,1024]{0,1:T(8,128)} fusion(bf16[1024,1024]{0,1:T(8,128)(2,1)S(1)} %fusion.3, bf16[4096,1024]{1,0:T(8,128)(2,1)} %param.5), kind=kOutput, calls=%fused_computation.1 | convolution fusion | flops 8589934592 | bytes 27262976 | tf_op jit(solution)/shard_map/dot_general | solution.py:25
  352.7 17.5 %copy.12 = f32[4096,1024]{1,0:T(8,128)} copy(f32[4096,1024]{0,1:T(8,128)} %convolution_bitcast_fusion.1) | data formatting | bytes 33554432
  370.2 0.0 copy-start.1
  370.2 0.0 reduce-scatter.7.cloned.1.call-update
  370.2 0.0 reduce-scatter.5.cloned.1.call-start
  370.2 1.5 copy-done.1
  371.8 14.5 %convolution_bitcast_fusion = f32[4096,1024]{0,1:T(8,128)} fusion(bf16[1024,1024]{0,1:T(8,128)(2,1)S(1)} %copy-done.1, bf16[1024,4096]{1,0:T(8,128)(2,1)} %param.4), kind=kOutput, calls=%fused_computation | convolution fusion | flops 8589934592 | bytes 27262976 | tf_op jit(solution)/shard_map/dot_general | solution.py:34
  386.3 0.0 reduce-scatter.5.cloned.1.call-update
  386.3 287.1 %reduce-scatter.7.cloned.1.call-done = f32[64,1024]{1,0:T(8,128)} async-done(((f32[4096,1024]{1,0:T(8,128)}), f32[64,1024]{1,0:T(8,128)}) %reduce-scatter.7.cloned.1.call-update) | async-done | bytes 262160
  673.4 1.1 copy.13
  674.6 0.8 copy.10
  675.3 195.6 %reduce-scatter.5.cloned.1.call-done = f32[2048,1024]{0,1:T(8,128)} async-done(((f32[4096,1024]{0,1:T(8,128)}), f32[2048,1024]{0,1:T(8,128)}) %reduce-scatter.5.cloned.1.call-update) | async-done | bytes 8388624 | tf_op jit(solution)/shard_map/reduce_scatter | solution.py:33
  871.0 6.0 convert_element_type.32
  876.9 6.4 copy.11
  (1 shorter events, 0.0 us)
Async XLA Ops:
  11.1 30.3 %all-to-all-start = ((bf16[2,1024,512]{1,2,0:T(8,128)(2,1)}), bf16[2,1024,512]{1,2,0:T(8,128)(2,1)S(1)}, u32[]{:S(2)}, u32[]{:S(2)}) async-start(bf16[2,1024,512]{1,2,0:T(8,128)(2,1)} %copy.9), calls=%async_computation | async-start | bytes 4194304 | tf_op jit(solution)/shard_map/all_to_all | solution.py:8
  16.0 657.5 %reduce-scatter.7.cloned.1.call-start = ((), (), s32[]{:S(2)}) async-start(), calls=%async_computation.4 | async-start | bytes 17039360
  31.1 302.3 %copy-start.2 = (f32[1024]{0:T(1024)S(1)}, f32[1024]{0:T(1024)}, u32[]{:S(2)}) copy-start(f32[1024]{0:T(1024)} %param.7) | copy-start | bytes 12292
  336.9 1.3 copy-start
  370.2 1.6 copy-start.1
  370.2 500.8 %reduce-scatter.5.cloned.1.call-start = ((), (), s32[]{:S(2)}) async-start(), calls=%async_computation.3 | async-start | bytes 25165824 | tf_op jit(solution)/shard_map/reduce_scatter | solution.py:33
Sparse Core Ops, SparseCore 0:
  370.3 303.0 reduce-scatter.6
  675.8 195.0 reduce-scatter.4
where the time goes:
time: 891 us; the launch traced here: 890 us
  waiting for transfers between devices  493 us (55%)
  blocking collectives  288 us (32%)
  matrix products  44.1 us (5%)
  local copies, waits for them, and re-layouts  32.6 us (4%)
  between operations  14.1 us (2%)
  other arithmetic  13.4 us (2%)
    unnamed x3, waiting for transfers between devices  287 us
    reduce_scatter x1, waiting for transfers between devices, per_device(): lax.psum_scatter(lax.dot_general(hidden_states, logit_grad, (((0,), (0,))...  196 us
    psum x1, blocking collectives, per_device(): lax.psum((student_total, teacher_total), ('vocab', 'dp'))  145 us
    pmax x1, blocking collectives, per_device(): lax.pmax((student_top, teacher_top), ('vocab', 'dp'))  143 us
    unnamed x10, local copies, waits for them, and re-layouts  28.6 us
  transfers between devices with their start and end apart: 3, of which 3 were waited for; matrix products, arithmetic and copies ran while one was open for 4% of the time, Pallas kernels for 0%

commit v1 on v0

--- a/solution.py
+++ b/solution.py
@@ -2,6 +2,9 @@
 import jax.numpy as jnp
 from jax import lax
 from jax.sharding import PartitionSpec as P
+from jax.lax import psum
+
+apply_the_shapes = lambda vals: psum(psum(vals, "vocab"), "dp")
 
 
 def per_device(hidden_states, head_weight, teacher_logits, token_weight):
@@ -14,7 +17,7 @@
     student_top, teacher_top = lax.pmax((student_top, teacher_top), ("vocab", "dp"))
     student_total = jnp.sum(jnp.exp(logits - student_top[:, None]), axis=1)
     teacher_total = jnp.sum(jnp.exp(teacher - teacher_top[:, None]), axis=1)
-    student_total, teacher_total = lax.psum((student_total, teacher_total), ("vocab", "dp"))
+    student_total, teacher_total = apply_the_shapes((student_total, teacher_total))
     student_norm = student_top + jnp.log(student_total)
     teacher_norm = teacher_top + jnp.log(teacher_total)
     logit_grad = (

time: 891 us -> 781 us (0.88)
  blocking collectives: 288 us -> 176 us
    psum x1 -> x2, blocking collectives: 145 us -> 33.5 us  [apply_the_shapes = lambda vals: psum(psum(vals, 'vocab'), 'dp')]
where the time goes in v1:
time: 781 us; the launch traced here: 780 us
  waiting for transfers between devices  495 us (63%)
  blocking collectives  176 us (23%)
  matrix products  44 us (6%)
  local copies, waits for them, and re-layouts  32.6 us (4%)
  between operations  14.1 us (2%)
  other arithmetic  13.4 us (2%)
    unnamed x3, waiting for transfers between devices  288 us
    reduce_scatter x1, waiting for transfers between devices, per_device(): lax.psum_scatter(lax.dot_general(hidden_states, logit_grad, (((0,), (0,))...  196 us
    pmax x1, blocking collectives, per_device(): lax.pmax((student_top, teacher_top), ('vocab', 'dp'))  143 us
    psum x2, blocking collectives, apply_the_shapes = lambda vals: psum(psum(vals, 'vocab'), 'dp')  33.5 us
    unnamed x10, local copies, waits for them, and re-layouts  28.6 us
  transfers between devices with their start and end apart: 3, of which 3 were waited for; matrix products, arithmetic and copies ran while one was open for 4% of the time, Pallas kernels for 0%

profile of v1, /device:TPU:1, one launch (start us, length us, event | category | flops | bytes accessed | tf_op | source)
XLA Modules:
  0.0 780.0 jit_solution(1549581924462197513)
XLA Ops:
  7.2 4.0 copy.9
  11.1 4.8 all-to-all-start
  16.0 0.0 reduce-scatter.7.cloned.1.call-start
  16.0 15.1 %fusion.4 = (f32[1024]{0:T(1024)S(1)}, f32[1024,1024]{0,1:T(8,128)}) fusion(bf16[1024,4096]{1,0:T(8,128)(2,1)} %param.4, bf16[4096,1024]{1,0:T(8,128)(2,1)} %param.5), kind=kOutput, calls=%fused_computation.12 | convolution fusion | flops 8590982144 | bytes 20975616 | tf_op jit(solution)/shard_map/dot_general | solution.py:14
  31.1 0.0 copy-start.2
  31.1 10.4 %all-to-all-done = bf16[2,1024,512]{1,2,0:T(8,128)(2,1)S(1)} async-done(((bf16[2,1024,512]{1,2,0:T(8,128)(2,1)}), bf16[2,1024,512]{1,2,0:T(8,128)(2,1)S(1)}, u32[]{:S(2)}, u32[]{:S(2)}) %all-to-all-start) | async-done | bytes 2097184 | tf_op jit(solution)/shard_map/all_to_all | solution.py:11
  41.4 0.4 reduce_max.24
  41.8 142.9 %all-reduce = (f32[1024]{0:T(1024)S(1)}, f32[1024]{0:T(1024)S(1)}) all-reduce(bf16[1024]{0:T(1024)(128)(2,1)S(1)} %reduce_max.24, f32[1024]{0:T(1024)S(1)} %get-tuple-element.12), channel_id=1, replica_groups=mesh['vocab'=8,'dp'=8,'teacher'=2] {'vocab','dp'}, use_global_device_ids=true, to_apply=%region_6.0 | all-reduce | flops 2048 | bytes 14336 | tf_op jit(solution)/shard_map/pmax | solution.py:17
  184.7 2.8 exponential_reduce_fusion.1
  187.6 0.7 exponential_reduce_fusion
  188.3 12.7 %all-reduce.2 = (f32[1024]{0:T(1024)S(1)}, f32[1024]{0:T(1024)S(1)}) all-reduce(f32[1024]{0:T(1024)S(1)} %exponential_reduce_fusion, f32[1024]{0:T(1024)S(1)} %exponential_reduce_fusion.1), channel_id=1, replica_groups=mesh['vocab'=8,'dp'=8,'teacher'=2] {'vocab'}, use_global_device_ids=true, to_apply=%region_8.0 | all-reduce | flops 2048 | bytes 16384 | tf_op jit(solution)/shard_map/psum | solution.py:7
  201.0 20.7 %all-reduce.1 = (f32[1024]{0:T(1024)S(1)}, f32[1024]{0:T(1024)S(1)}) all-reduce(f32[1024]{0:T(1024)S(1)} %get-tuple-element.10, f32[1024]{0:T(1024)S(1)} %get-tuple-element.11), channel_id=1, replica_groups=mesh['vocab'=8,'dp'=8,'teacher'=2] {'dp'}, use_global_device_ids=true, to_apply=%region_9.0 | all-reduce | flops 2048 | bytes 16384 | tf_op jit(solution)/shard_map/psum | solution.py:7
  221.8 0.0 copy-done.2
  221.8 3.5 fusion.3
  225.3 0.0 copy-start
  225.3 1.3 copy-done
  226.6 14.5 %convolution_bitcast_fusion.1 = f32[4096,1024]{0,1:T(8,128)} fusion(bf16[1024,1024]{0,1:T(8,128)(2,1)S(1)} %fusion.3, bf16[4096,1024]{1,0:T(8,128)(2,1)} %param.5), kind=kOutput, calls=%fused_computation.1 | convolution fusion | flops 8589934592 | bytes 27262976 | tf_op jit(solution)/shard_map/dot_general | solution.py:28
  241.1 17.5 %copy.12 = f32[4096,1024]{1,0:T(8,128)} copy(f32[4096,1024]{0,1:T(8,128)} %convolution_bitcast_fusion.1) | data formatting | bytes 33554432
  258.6 0.0 copy-start.1
  258.6 0.0 reduce-scatter.7.cloned.1.call-update
  258.6 0.0 reduce-scatter.5.cloned.1.call-start
  258.6 1.5 copy-done.1
  260.2 14.4 %convolution_bitcast_fusion = f32[4096,1024]{0,1:T(8,128)} fusion(bf16[1024,1024]{0,1:T(8,128)(2,1)S(1)} %copy-done.1, bf16[1024,4096]{1,0:T(8,128)(2,1)} %param.4), kind=kOutput, calls=%fused_computation | convolution fusion | flops 8589934592 | bytes 27262976 | tf_op jit(solution)/shard_map/dot_general | solution.py:37
  274.5 0.0 reduce-scatter.5.cloned.1.call-update
  274.6 287.9 %reduce-scatter.7.cloned.1.call-done = f32[64,1024]{1,0:T(8,128)} async-done(((f32[4096,1024]{1,0:T(8,128)}), f32[64,1024]{1,0:T(8,128)}) %reduce-scatter.7.cloned.1.call-update) | async-done | bytes 262160
  562.4 1.1 copy.13
  563.5 0.8 copy.10
  564.3 196.5 %reduce-scatter.5.cloned.1.call-done = f32[2048,1024]{0,1:T(8,128)} async-done(((f32[4096,1024]{0,1:T(8,128)}), f32[2048,1024]{0,1:T(8,128)}) %reduce-scatter.5.cloned.1.call-update) | async-done | bytes 8388624 | tf_op jit(solution)/shard_map/reduce_scatter | solution.py:36
  760.8 6.0 convert_element_type.32
  766.8 6.4 copy.11
  (1 shorter events, 0.0 us)
Async XLA Ops:
  11.1 30.3 %all-to-all-start = ((bf16[2,1024,512]{1,2,0:T(8,128)(2,1)}), bf16[2,1024,512]{1,2,0:T(8,128)(2,1)S(1)}, u32[]{:S(2)}, u32[]{:S(2)}) async-start(bf16[2,1024,512]{1,2,0:T(8,128)(2,1)} %copy.9), calls=%async_computation | async-start | bytes 4194304 | tf_op jit(solution)/shard_map/all_to_all | solution.py:11
  16.0 546.5 %reduce-scatter.7.cloned.1.call-start = ((), (), s32[]{:S(2)}) async-start(), calls=%async_computation.4 | async-start | bytes 17039360
  31.1 190.7 %copy-start.2 = (f32[1024]{0:T(1024)S(1)}, f32[1024]{0:T(1024)}, u32[]{:S(2)}) copy-start(f32[1024]{0:T(1024)} %param.7) | copy-start | bytes 12292
  225.3 1.3 copy-start
  258.6 1.6 copy-start.1
  258.6 502.2 %reduce-scatter.5.cloned.1.call-start = ((), (), s32[]{:S(2)}) async-start(), calls=%async_computation.3 | async-start | bytes 25165824 | tf_op jit(solution)/shard_map/reduce_scatter | solution.py:36
Sparse Core Ops, SparseCore 0:
  258.7 303.6 reduce-scatter.6
  564.8 195.9 reduce-scatter.4
